TPU v7x, 32 devices: a whole 2x2x4 slice. The times are simulated.
32 devices in a mesh: batch: 2 (over y), freq: 8 (over z, x), elem: 2 (over core).
Axes of the slice: x: 2, y: 2, z: 4, core: 2. Of those that a mesh axis runs over, the one named last changes fastest.
Arguments:
- flaw_cells: int32 [512], P('batch'), parts along dimension 0, may hold values from 0 to 255, each once
- flaw_blocks: int32 [16], P('batch'), parts along dimension 0, may hold values from 0 to 7, each once
- element_channel: int32 [256], P('elem'), may hold values from 0 to 255, each once
- focal_delay: float32 [256, 256], replicated, may hold values from 0 to 64
- beam_field: bfloat16 [128, 2, 256, 256], P('freq', None, 'elem'), may hold values from -0.125 to 0.125
- flaw_size: float32 [4, 128], P('batch'), parts along dimension 0, may hold values from 0.5 to 4
- flaw_slope: float32 [4, 128], P('batch'), parts along dimension 0, may hold values from 0.2 to 1
- noise_level: float32 [4, 128], P(('batch', 'elem'), 'freq'), parts along dimension 0, may hold values from 0.5 to 5
Outputs:
- flaw_peak: float32 [4, 128], P(('batch', 'elem'), 'freq'), parts along dimension 0
- detection: float32 [4, 128], P(('batch', 'elem'), 'freq'), parts along dimension 0
There are 2 independent parts, one for each index of `batch`. A program takes and returns all parts, laid end to end along the dimension named above; an argument that names none is the same for every part. Nothing has to cross between parts.
Inputs may be any that keep to these rules, and one draw needn't show every extreme that they name: `flaw_cells`: every site holds exactly one flaw. `flaw_blocks`: every scan block belongs to exactly one flaw group. `element_channel`: every channel drives exactly one element.
All inputs are finite; a program needn't handle non-finite values.
Results may differ from a plain program's by a relative error of at most 0.0011.
Values may be sent and summed in bfloat16 or wider, within the bound.
A program may use at most 64 MiB of HBM per device.

v0:
```python
import math
import jax
import jax.numpy as jnp
from jax import lax
from jax.sharding import PartitionSpec as P

W_DEV = 16
FG = 128
NB = 4
SB = 32
T_CAP = 1024
EDGE = 0.6
STEEP = 3.0
EPS = 1e-05


def kirchhoff(angular, flaw_size, flaw_slope):
    angles = angular[None, :, None] * (2.0 * flaw_size * flaw_slope)[:, None, :]
    real_part = flaw_size[:, None, :] * (1.0 + EDGE) * jnp.cos(angles)
    imag_part = flaw_size[:, None, :] * (EDGE - 1.0) * jnp.sin(angles)
    return (real_part, imag_part)


def focal_law(angular, delays):
    phases = angular[:, None, None, None] * delays[None]
    return jnp.concatenate([jnp.cos(phases), -jnp.sin(phases)], axis=-1).astype(jnp.bfloat16)


def field_matrix(fields):
    real_part = fields[:, 0]
    imag_part = fields[:, 1]
    upper_rows = jnp.concatenate([real_part, imag_part], axis=-1)
    lower_rows = jnp.concatenate([-imag_part, real_part], axis=-1)
    return jnp.concatenate([upper_rows, lower_rows], axis=1)


def combine(product, k_real, k_imag):
    columns = k_real.shape[-1]
    real_part = product[..., :columns]
    imag_part = product[..., columns:]
    scale_real = k_real[:, :, None, :]
    scale_imag = k_imag[:, :, None, :]
    return jnp.stack(
        [
            scale_real * real_part - scale_imag * imag_part,
            scale_real * imag_part + scale_imag * real_part,
        ],
        axis=2,
    )


def envelope_peak(spectra, row_count):
    groups, freq_total, planes, columns = spectra.shape
    sample_count = min(T_CAP, 2 * freq_total)
    time_block = min(128, sample_count)
    freq_index = jnp.arange(freq_total, dtype=jnp.int32)
    scaling = 1.0 / math.sqrt(freq_total)

    def advance(step_index, running):
        sample_times = step_index * time_block + jnp.arange(time_block, dtype=jnp.int32)
        phase_steps = freq_index[:, None] * sample_times[None, :] % (2 * freq_total)
        angles = phase_steps.astype(jnp.float32) * (math.pi / freq_total)
        cosine = jnp.cos(angles)
        sine_part = jnp.sin(angles)
        twiddle = jnp.stack(
            [jnp.stack([cosine, sine_part], axis=1), jnp.stack([-sine_part, cosine], axis=1)],
            axis=1,
        )
        twiddle_high = lax.optimization_barrier(twiddle.astype(jnp.bfloat16))
        twiddle_low = (twiddle - twiddle_high.astype(jnp.float32)).astype(jnp.bfloat16)
        signal = jnp.einsum(
            "gwcx,wckt->gkxt", spectra, twiddle_high, preferred_element_type=jnp.float32
        )
        signal = signal + jnp.einsum(
            "gwcx,wckt->gkxt", spectra, twiddle_low, preferred_element_type=jnp.float32
        )
        signal = signal * scaling
        magnitude = jnp.sqrt(signal[:, 0] * signal[:, 0] + signal[:, 1] * signal[:, 1])
        magnitude = magnitude.reshape(groups, row_count, columns // row_count, time_block)
        return jnp.maximum(running, jnp.max(magnitude, axis=(1, 3)))

    initial = jnp.zeros((groups, columns // row_count), jnp.float32)
    return lax.fori_loop(0, sample_count // time_block, advance, initial)


def regroup_peaks(moved):
    groups, freq_total, planes, row_count, flaw_count = moved.shape
    return envelope_peak(
        moved.reshape(groups, freq_total, planes, row_count * flaw_count), row_count
    )


def body(
    flaw_cells,
    flaw_blocks,
    element_channel,
    focal_delay,
    beam_field,
    flaw_size,
    flaw_slope,
    noise_level,
):
    freq_count = lax.axis_size("freq")
    freq_total = W_DEV * freq_count
    group_total = flaw_size.shape[0]
    row_total = NB * SB
    first_freq = lax.axis_index("freq") * W_DEV
    angular = (first_freq + jnp.arange(W_DEV, dtype=jnp.int32)).astype(jnp.float32) * (
        math.pi / freq_total
    )
    scan_rows = (
        flaw_blocks.reshape(group_total, NB)[:, :, None] * SB
        + jnp.arange(SB, dtype=jnp.int32)[None, None, :]
    ).reshape(group_total, row_total)
    delays = jnp.moveaxis(
        jnp.take(jnp.take(focal_delay, element_channel, axis=0), scan_rows, axis=1), 0, 2
    )
    fields = jnp.take(beam_field, flaw_cells, axis=3).reshape(
        W_DEV, 2, element_channel.shape[0], group_total, FG
    )
    k_real, k_imag = kirchhoff(angular, flaw_size, flaw_slope)
    focal_terms = focal_law(angular, delays)
    field_terms = field_matrix(fields)
    product = jnp.einsum(
        "wgre,wegf->gwrf", focal_terms, field_terms, preferred_element_type=jnp.float32
    )
    partial_value = combine(product, k_real, k_imag).astype(jnp.bfloat16)
    rounded_term = lax.optimization_barrier(partial_value).astype(jnp.float32)
    summed = lax.psum_scatter(
        rounded_term.astype(jnp.bfloat16), "elem", scatter_dimension=0, tiled=True
    )
    partial_peak = regroup_peaks(
        lax.all_to_all(summed, "freq", split_axis=3, concat_axis=1, tiled=True)
    )
    whole_peak = lax.pmax(partial_peak, "freq")
    columns = FG // freq_count
    flaw_peak = lax.dynamic_slice_in_dim(whole_peak, lax.axis_index("freq") * columns, columns, 1)
    detection = jax.nn.sigmoid(STEEP * (jnp.log(flaw_peak + EPS) - jnp.log(noise_level)))
    return (flaw_peak, detection)


def solution(mesh):
    in_specs = (
        P("batch"),
        P("batch"),
        P("elem"),
        P(),
        P("freq", None, "elem", None),
        P("batch", None),
        P("batch", None),
        P(("batch", "elem"), "freq"),
    )
    out_specs = (P(("batch", "elem"), "freq"), P(("batch", "elem"), "freq"))
    return jax.shard_map(body, mesh=mesh, in_specs=in_specs, out_specs=out_specs, check_vma=False)
```

profile of v0, /device:TPU:0, one launch (start us, length us, event | category | flops | bytes accessed | tf_op | source)
XLA Modules:
  0.0 130.7 jit_solution(10028995258592045228)
XLA Ops:
  7.2 0.7 compare_select_fusion.3
  7.9 1.2 compare_and_fusion
  9.1 0.7 broadcast_multiply_fusion.2
  10.1 0.7 compare_select_fusion
  10.8 0.7 and_bitcast_fusion
  11.4 3.5 %copy.28 = bf16[16,2,128,256]{2,0,3,1:T(8,128)(2,1)S(1)} copy(bf16[16,2,128,256]{3,2,1,0:T(8,128)(2,1)} %param.14) | data formatting | bytes 4194304 | tf_op args[4]
  14.9 2.3 %gather_fusion.2 = bf16[256,16,2,128]{3,1,2,0:T(8,128)(2,1)} fusion(bf16[16,2,128,256]{2,0,3,1:T(8,128)(2,1)S(1)} %copy.28, s32[1024]{0:T(1024)S(1)} %pad_clamp_fusion), kind=kCustom, calls=%fused_computation.2 | custom fusion | bytes 4195328 | tf_op jit(solution)/shard_map/jit(_take)/gather | solution.py:118
  17.2 3.5 %copy.30 = bf16[16,2,128,2,128]{4,2,0,3,1:T(8,128)(2,1)S(1)} copy(bf16[16,2,128,2,128]{2,0,1,4,3:T(8,128)(2,1)} %bitcast.85) | data formatting | bytes 4194304 | tf_op jit(solution)/shard_map/jit(_take)/gather | solution.py:118
  21.3 0.8 gather_fusion
  22.1 1.4 %broadcast_select_fusion.3 = f32[128,256]{1,0:T(8,128)} fusion(f32[128,256]{1,0:T(8,128)S(1)} %gather_fusion, pred[128]{0:T(512)(128)(4,1)} %compare_and_fusion), kind=kLoop, calls=%fused_computation.64 | loop fusion | flops 32768 | bytes 262272 | tf_op jit(solution)/shard_map/jit(_take)/select_n | solution.py:116
  23.5 1.0 copy.27
  25.0 1.3 %gather_fusion.1 = f32[256,128]{1,0:T(8,128)} fusion(f32[128,256]{0,1:T(8,128)S(1)} %copy.27, s32[1024]{0:T(1024)S(1)} %pad_clamp_fusion.1), kind=kCustom, calls=%fused_computation.1 | custom fusion | bytes 263168 | tf_op jit(solution)/shard_map/jit(_take)/gather | solution.py:116
  26.3 1.0 broadcast_select_fusion.2
  27.3 7.8 %fusion.30 = (bf16[16,2,128,128]{3,2,0,1:T(8,128)(2,1)S(1)}, bf16[16,2,128,128]{3,2,0,1:T(8,128)(2,1)S(1)}) fusion(f32[2,128,128]{2,1,0:T(8,128)S(1)} %broadcast_select_fusion.2, f32[16]{0:T(128)S(1)} %convert_multiply_fusion), kind=kLoop, calls=%fused_computation.49 | loop fusion | flops 2097152 | bytes 2228288 | tf_op jit(solution)/shard_map/convert.4
  35.1 0.7 broadcast_multiply_fusion.1
  36.0 1.4 %fusion.22 = f32[2,16,128,256]{3,2,1,0:T(8,128)S(1)} fusion(bf16[16,128,2,128]{3,1,0,2:T(8,128)(2,1)S(1)} %get-tuple-element.144, bf16[16,128,2,128]{3,1,0,2:T(8,128)(2,1)S(1)} %fusion.42, bf16[16,128,2,128]{3,1,0,2:T(8,128)(2,1)S(1)} %get-tuple-element.143, bf16[16,2,128,128]{3,2,0,1:T(8,128)(2,1)S(1)} %get-tuple-element.146, ...), kind=kOutput, calls=%fused_computation.39 | convolution fusion | flops 557842432 | bytes 9437184 | tf_op jit(solution)/shard_map/wgre,wegf->gwrf/dot_general | solution.py:124
  38.1 1.5 %pad_maximum_fusion.1 = bf16[2,16,2,128,128]{4,3,1,0,2:T(8,128)(2,1)} fusion(bf16[2,16,1,128,128]{4,3,1,0,2:T(8,128)(2,1)S(1)} %get-tuple-element.142, bf16[2,16,1,128,128]{4,3,1,0,2:T(8,128)(2,1)S(1)} %get-tuple-element.141), kind=kLoop, calls=%fused_computation.55 | loop fusion | flops 1048576 | bytes 4194304 | tf_op jit(solution)/shard_map/stack | solution.py:43
  40.8 22.9 %all-reduce.3.cloned.1.call-done = bf16[2,16,2,128,128]{4,3,1,0,2:T(8,128)(2,1)} async-done(((bf16[2,16,2,128,128]{4,3,1,0,2:T(8,128)(2,1)}), bf16[2,16,2,128,128]{4,3,1,0,2:T(8,128)(2,1)}) %all-reduce.3.cloned.1.call-update) | async-done | bytes 2097168
  63.6 1.9 %constant_dynamic-slice_fusion = bf16[1,16,2,128,128]{4,3,1,0,2:T(8,128)(2,1)S(1)} fusion(bf16[2,16,2,128,128]{4,3,1,0,2:T(8,128)(2,1)} %all-reduce.3.cloned.1.call-done, u32[]{:T(128)} %bitcast.34), kind=kLoop, calls=%fused_computation.81 | loop fusion | bytes 2097156
  65.6 1.7 %copy.31 = bf16[1,16,2,128,128]{4,1,0,2,3:T(8,128)(2,1)} copy(bf16[1,16,2,128,128]{4,3,1,0,2:T(8,128)(2,1)S(1)} %constant_dynamic-slice_fusion) | data formatting | bytes 2097152 | tf_op jit(solution)/shard_map/reduce_scatter | solution.py:129
  67.2 5.8 %all-to-all-start = ((bf16[1,16,2,128,128]{4,1,0,2,3:T(8,128)(2,1)}), bf16[1,16,2,128,128]{4,1,0,2,3:T(8,128)(2,1)S(1)}, u32[]{:S(2)}, u32[]{:S(2)}) async-start(bf16[1,16,2,128,128]{4,1,0,2,3:T(8,128)(2,1)} %copy.31), calls=%async_computation | async-start | bytes 2097152 | tf_op jit(solution)/shard_map/all_to_all | solution.py:133
  73.0 26.2 %all-to-all-done = bf16[1,16,2,128,128]{4,1,0,2,3:T(8,128)(2,1)S(1)} async-done(((bf16[1,16,2,128,128]{4,1,0,2,3:T(8,128)(2,1)}), bf16[1,16,2,128,128]{4,1,0,2,3:T(8,128)(2,1)S(1)}, u32[]{:S(2)}, u32[]{:S(2)}) %all-to-all-start) | async-done | bytes 1048608 | tf_op jit(solution)/shard_map/all_to_all | solution.py:133
  100.2 3.5 %while.16 = (s32[]{:T(128)}, f32[1,128]{1,0:T(1,128)S(1)}, bf16[1,128,2,2048]{3,1,2,0:T(8,128)(2,1)S(1)}, s32[]{:T(128)}, s32[]{:T(128)}, /*index=5*/s32[]{:T(128)}) while((s32[]{:T(128)}, f32[1,128]{1,0:T(1,128)S(1)}, bf16[1,128,2,2048]{3,1,2,0:T(8,128)(2,1)S(1)}, s32[]{:T(128)}, s32[]{:T(128)}, /*index=5*/s32[]{:T(128)}) %tuple.58), condition=%wide.region_4.5_spmd.clone, body=%wide.region_1.4_spmd.clone.sunk | while | flops 539607296 | bytes 12078175 | solution.py:83
  103.7 19.5 %pmax.7 = f32[1,128]{1,0:T(1,128)S(1)} all-reduce(f32[1,128]{1,0:T(1,128)S(1)} %get-tuple-element.113), channel_id=1, replica_groups=mesh['batch'=2,'freq'=8,'elem'=2] {'freq'}, use_global_device_ids=true, to_apply=%region_5.6 | all-reduce | flops 128 | bytes 1024 | tf_op jit(solution)/shard_map/pmax | solution.py:135
  (48 shorter events, 8.4 us)
Async XLA Ops:
  7.2 14.1 %copy-start = (f32[256,256]{1,0:T(8,128)S(1)}, f32[256,256]{1,0:T(8,128)}, u32[]{:S(2)}) copy-start(f32[256,256]{1,0:T(8,128)} %param.13) | copy-start | bytes 786436
  7.2 56.5 %all-reduce.3.cloned.1.call-start = ((), (), s32[]{:S(2)}) async-start(), calls=%async_computation.1 | async-start | bytes 4194304
  39.5 0.7 copy-start.2
  67.2 32.0 %all-to-all-start = ((bf16[1,16,2,128,128]{4,1,0,2,3:T(8,128)(2,1)}), bf16[1,16,2,128,128]{4,1,0,2,3:T(8,128)(2,1)S(1)}, u32[]{:S(2)}, u32[]{:S(2)}) async-start(bf16[1,16,2,128,128]{4,1,0,2,3:T(8,128)(2,1)} %copy.31), calls=%async_computation | async-start | bytes 2097152 | tf_op jit(solution)/shard_map/all_to_all | solution.py:133
  100.2 23.0 %copy-start.1 = (f32[1,16]{1,0:T(1,128)S(1)}, f32[1,16]{1,0:T(1,128)}, u32[]{:S(2)}) copy-start(f32[1,16]{1,0:T(1,128)} %param.17) | copy-start | bytes 196
Sparse Core Ops, SparseCore 0:
  39.7 23.9 all-reduce.2
where the time goes:
time: 131 us
  waiting for transfers between devices  49.1 us (37%)
  other arithmetic  20.2 us (15%)
  blocking collectives  19.5 us (15%)
  local copies, waits for them, and re-layouts  18.6 us (14%)
  between operations  14.2 us (11%)
  starting transfers between devices  5.81 us (4%)
  matrix products  3.2 us (2%)
    all_to_all x1, waiting for transfers between devices, body(): lax.all_to_all(summed, 'freq', split_axis=3, concat_axis=1, tiled=True)  26.2 us
    unnamed x2, waiting for transfers between devices  22.9 us
    pmax x1, blocking collectives, body(): whole_peak = lax.pmax(partial_peak, 'freq')  19.5 us
    another operation x1, other arithmetic  7.81 us
    unnamed x9, local copies, waits for them, and re-layouts  6.63 us
    all_to_all x1, starting transfers between devices, body(): lax.all_to_all(summed, 'freq', split_axis=3, concat_axis=1, tiled=True)  5.78 us
    gather x2, local copies, waits for them, and re-layouts, body(): jnp.take(beam_field, flaw_cells, axis=3)  5.75 us
  transfers between devices with their start and end apart: 2, of which 2 were waited for; matrix products, arithmetic and copies ran while one was open for 0% of the time, Pallas kernels for 0%

commit v1 on v0

--- a/solution.py
+++ b/solution.py
@@ -1,3 +1,4 @@
+import functools
 import math
 import jax
 import jax.numpy as jnp
@@ -12,6 +13,42 @@
 EDGE = 0.6
 STEEP = 3.0
 EPS = 1e-05
+
+
+def end_joints(raw, out_dim, in_array):
+    g_now, w1 = (raw.shape[:out_dim], raw.shape[out_dim + 1 :])
+    return jnp.moveaxis(raw.reshape(*g_now, in_array, -1, *w1), out_dim, 0)
+
+
+def time_the_values(unit, row_dim):
+    unit = jnp.moveaxis(unit, 0, row_dim)
+    wide_out = unit.shape
+    return unit.reshape(
+        *wide_out[:row_dim], wide_out[row_dim] * wide_out[row_dim + 1], *wide_out[row_dim + 2 :]
+    )
+
+
+def name_zones(local_values, axis_key, xin, frame_in):
+    parts_out = lax.axis_size(axis_key)
+    current_block, small = (parts_out, lax.axis_index(axis_key))
+    b_now = end_joints(local_values, xin, current_block)
+    i0 = 1
+    frames = [b_now[small]]
+    while i0 < current_block:
+        f_now = b_now[(small + i0) % current_block]
+        frames.append(
+            lax.ppermute(
+                f_now,
+                axis_name=axis_key,
+                perm=[(s, (s + i0) % current_block) for s in range(current_block)],
+            )
+        )
+        i0 = i0 + 1
+    b_now = jnp.stack(frames)[(small - jnp.arange(current_block)) % current_block]
+    return time_the_values(b_now, frame_in)
+
+
+save_pools = functools.partial(name_zones, axis_key="freq", xin=3, frame_in=1)
 
 
 def kirchhoff(angular, flaw_size, flaw_slope):
@@ -129,9 +166,7 @@
     summed = lax.psum_scatter(
         rounded_term.astype(jnp.bfloat16), "elem", scatter_dimension=0, tiled=True
     )
-    partial_peak = regroup_peaks(
-        lax.all_to_all(summed, "freq", split_axis=3, concat_axis=1, tiled=True)
-    )
+    partial_peak = regroup_peaks(save_pools(summed))
     whole_peak = lax.pmax(partial_peak, "freq")
     columns = FG // freq_count
     flaw_peak = lax.dynamic_slice_in_dim(whole_peak, lax.axis_index("freq") * columns, columns, 1)

time: 131 us -> 126 us (0.962)
  waiting for transfers between devices: 49.1 us -> 30 us
  blocking collectives: 19.5 us -> 27.7 us
  starting transfers between devices: 5.81 us -> 13.2 us
  other arithmetic: 20.2 us -> 18.2 us
    all_to_all x1 -> x0, waiting for transfers between devices: 26.2 us -> none  [body(): lax.all_to_all(summed, 'freq', split_axis=3, concat_axis=1, tiled=True)]
    ppermute x0 -> x7, starting transfers between devices: none -> 13.1 us  [name_zones(): lax.ppermute(f_now, axis_name=axis_key, perm=[(s, (s + i0) % current_bloc...]
    pmax x1, blocking collectives: 19.5 us -> 27.7 us  [body(): whole_peak = lax.pmax(partial_peak, 'freq')]
    ppermute x0 -> x7, waiting for transfers between devices: none -> 7.18 us  [name_zones(): lax.ppermute(f_now, axis_name=axis_key, perm=[(s, (s + i0) % current_bloc...]
    all_to_all x1 -> x0, starting transfers between devices: 5.78 us -> none  [body(): lax.all_to_all(summed, 'freq', split_axis=3, concat_axis=1, tiled=True)]
    reduce_scatter x1 -> x0, local copies, waits for them, and re-layouts: 1.65 us -> none  [body(): lax.psum_scatter(rounded_term.astype(jnp.bfloat16), 'elem', scatter_dimen...]
    unnamed x9 -> x28, local copies, waits for them, and re-layouts: 6.63 us -> 7.59 us
  transfers between devices with their start and end apart: 2 -> 8, of which waited for: 2 -> 3; matrix products, arithmetic and copies ran while one was open for 0% -> 1% of each run, Pallas kernels for 0% -> 0%
where the time goes in v1:
time: 126 us; the launch traced here: 125 us
  waiting for transfers between devices  30 us (24%)
  blocking collectives  27.7 us (22%)
  local copies, waits for them, and re-layouts  18.3 us (15%)
  other arithmetic  18.2 us (14%)
  between operations  14.4 us (11%)
  starting transfers between devices  13.2 us (10%)
  matrix products  3.2 us (3%)
    pmax x1, blocking collectives, body(): whole_peak = lax.pmax(partial_peak, 'freq')  27.7 us
    unnamed x2, waiting for transfers between devices  22.9 us
    ppermute x7, starting transfers between devices, name_zones(): lax.ppermute(f_now, axis_name=axis_key, perm=[(s, (s + i0) % current_bloc...  13.1 us
    another operation x1, other arithmetic  7.81 us
    unnamed x28, local copies, waits for them, and re-layouts  7.59 us
    ppermute x7, waiting for transfers between devices, name_zones(): lax.ppermute(f_now, axis_name=axis_key, perm=[(s, (s + i0) % current_bloc...  7.18 us
    gather x2, local copies, waits for them, and re-layouts, body(): jnp.take(beam_field, flaw_cells, axis=3)  5.75 us
  transfers between devices with their start and end apart: 8, of which 3 were waited for; matrix products, arithmetic and copies ran while one was open for 1% of the time, Pallas kernels for 0%

profile of v1, /device:TPU:0, one launch (start us, length us, event | category | flops | bytes accessed | tf_op | source)
XLA Modules:
  0.0 125.2 jit_solution(14663995993420371712)
XLA Ops:
  8.6 3.5 %copy.42 = bf16[16,2,128,256]{2,0,3,1:T(8,128)(2,1)S(1)} copy(bf16[16,2,128,256]{3,2,1,0:T(8,128)(2,1)} %param.14) | data formatting | bytes 4194304 | tf_op args[4]
  12.5 2.3 %gather_fusion.2 = bf16[256,16,2,128]{3,1,2,0:T(8,128)(2,1)} fusion(bf16[16,2,128,256]{2,0,3,1:T(8,128)(2,1)S(1)} %copy.42, s32[1024]{0:T(1024)S(1)} %get-tuple-element.169), kind=kCustom, calls=%fused_computation.2 | custom fusion | bytes 4195328 | tf_op jit(solution)/shard_map/jit(_take)/gather | solution.py:155
  14.8 3.5 %copy.44 = bf16[16,2,128,2,128]{4,2,0,3,1:T(8,128)(2,1)S(1)} copy(bf16[16,2,128,2,128]{2,0,1,4,3:T(8,128)(2,1)} %bitcast.123) | data formatting | bytes 4194304 | tf_op jit(solution)/shard_map/jit(_take)/gather | solution.py:155
  19.9 0.8 gather_fusion
  20.6 1.4 %broadcast_select_fusion.3 = f32[128,256]{1,0:T(8,128)} fusion(f32[128,256]{1,0:T(8,128)S(1)} %gather_fusion, pred[128]{0:T(512)(128)(4,1)} %compare_and_fusion), kind=kLoop, calls=%fused_computation.81 | loop fusion | flops 32768 | bytes 262272 | tf_op jit(solution)/shard_map/jit(_take)/select_n | solution.py:153
  22.0 1.0 copy.41
  23.5 1.3 %gather_fusion.1 = f32[256,128]{1,0:T(8,128)} fusion(f32[128,256]{0,1:T(8,128)S(1)} %copy.41, s32[1024]{0:T(1024)S(1)} %get-tuple-element.170), kind=kCustom, calls=%fused_computation.1 | custom fusion | bytes 263168 | tf_op jit(solution)/shard_map/jit(_take)/gather | solution.py:153
  24.9 1.0 broadcast_select_fusion.2
  25.9 7.8 %fusion.30 = (bf16[16,2,128,128]{3,2,0,1:T(8,128)(2,1)S(1)}, bf16[16,2,128,128]{3,2,0,1:T(8,128)(2,1)S(1)}) fusion(f32[2,128,128]{2,1,0:T(8,128)S(1)} %broadcast_select_fusion.2, f32[16]{0:T(128)S(1)} %convert_multiply_fusion), kind=kLoop, calls=%fused_computation.50 | loop fusion | flops 2097152 | bytes 2228288 | tf_op jit(solution)/shard_map/convert.4
  34.6 1.4 %fusion.22 = f32[2,16,128,256]{3,2,1,0:T(8,128)S(1)} fusion(bf16[16,128,2,128]{3,1,0,2:T(8,128)(2,1)S(1)} %get-tuple-element.153, bf16[16,128,2,128]{3,1,0,2:T(8,128)(2,1)S(1)} %fusion.45, bf16[16,128,2,128]{3,1,0,2:T(8,128)(2,1)S(1)} %get-tuple-element.152, bf16[16,2,128,128]{3,2,0,1:T(8,128)(2,1)S(1)} %get-tuple-element.163, ...), kind=kOutput, calls=%fused_computation.40 | convolution fusion | flops 557842432 | bytes 9437184 | tf_op jit(solution)/shard_map/wgre,wegf->gwrf/dot_general | solution.py:161
  36.6 1.5 %pad_maximum_fusion.1 = bf16[2,16,2,128,128]{4,3,1,0,2:T(8,128)(2,1)} fusion(bf16[2,16,1,128,128]{4,3,1,0,2:T(8,128)(2,1)S(1)} %get-tuple-element.151, bf16[2,16,1,128,128]{4,3,1,0,2:T(8,128)(2,1)S(1)} %get-tuple-element.150), kind=kLoop, calls=%fused_computation.56 | loop fusion | flops 1048576 | bytes 4194304 | tf_op jit(solution)/shard_map/stack | solution.py:80
  39.4 22.8 %all-reduce.3.cloned.1.call-done = bf16[2,16,2,128,128]{4,3,1,0,2:T(8,128)(2,1)} async-done(((bf16[2,16,2,128,128]{4,3,1,0,2:T(8,128)(2,1)}), bf16[2,16,2,128,128]{4,3,1,0,2:T(8,128)(2,1)}) %all-reduce.3.cloned.1.call-update) | async-done | bytes 2097168
  62.2 1.9 %constant_dynamic-slice_fusion.9 = bf16[1,16,2,128,128]{4,3,1,0,2:T(8,128)(2,1)S(1)} fusion(bf16[2,16,2,128,128]{4,3,1,0,2:T(8,128)(2,1)} %all-reduce.3.cloned.1.call-done, u32[]{:T(128)} %bitcast.50), kind=kLoop, calls=%fused_computation.114 | loop fusion | bytes 2097156
  64.5 1.8 %collective-permute-start = (bf16[1,16,2,16,128]{4,3,2,1,0:T(8,128)(2,1)S(1)}, bf16[1,16,2,16,128]{4,3,2,1,0:T(8,128)(2,1)S(1)}, u32[]{:S(2)}, u32[]{:S(2)}) collective-permute-start(bf16[1,16,2,16,128]{4,3,2,1,0:T(8,128)(2,1)S(1)} %bitcast.133), channel_id=1, source_target_pairs={{0,2},{2,4},{4,6},{6,8},{8,10},{10,12},{12,14},{14,0},{1,3},{3,5},... | collective-permute-start | bytes 393224 | tf_op jit(solution)/shard_map/ppermute | solution.py:40
  66.3 1.5 %collective-permute-start.1 = (bf16[1,16,2,16,128]{4,3,2,1,0:T(8,128)(2,1)S(1)}, bf16[1,16,2,16,128]{4,3,2,1,0:T(8,128)(2,1)S(1)}, u32[]{:S(2)}, u32[]{:S(2)}) collective-permute-start(bf16[1,16,2,16,128]{4,3,2,1,0:T(8,128)(2,1)S(1)} %bitcast.132), channel_id=1, source_target_pairs={{0,4},{2,6},{4,8},{6,10},{8,12},{10,14},{12,0},{14,2},{1,5},{3,7},... | collective-permute-start | bytes 393224 | tf_op jit(solution)/shard_map/ppermute | solution.py:40
  67.8 2.5 %collective-permute-start.2 = (bf16[1,16,2,16,128]{4,3,2,1,0:T(8,128)(2,1)S(1)}, bf16[1,16,2,16,128]{4,3,2,1,0:T(8,128)(2,1)S(1)}, u32[]{:S(2)}, u32[]{:S(2)}) collective-permute-start(bf16[1,16,2,16,128]{4,3,2,1,0:T(8,128)(2,1)S(1)} %bitcast.131), channel_id=1, source_target_pairs={{0,6},{2,8},{4,10},{6,12},{8,14},{10,0},{12,2},{14,4},{1,7},{3,9},... | collective-permute-start | bytes 393224 | tf_op jit(solution)/shard_map/ppermute | solution.py:40
  70.3 1.5 %collective-permute-start.3 = (bf16[1,16,2,16,128]{4,3,2,1,0:T(8,128)(2,1)S(1)}, bf16[1,16,2,16,128]{4,3,2,1,0:T(8,128)(2,1)S(1)}, u32[]{:S(2)}, u32[]{:S(2)}) collective-permute-start(bf16[1,16,2,16,128]{4,3,2,1,0:T(8,128)(2,1)S(1)} %bitcast.130), channel_id=1, source_target_pairs={{0,8},{2,10},{4,12},{6,14},{8,0},{10,2},{12,4},{14,6},{1,9},{3,11}... | collective-permute-start | bytes 393224 | tf_op jit(solution)/shard_map/ppermute | solution.py:40
  71.8 2.5 %collective-permute-start.4 = (bf16[1,16,2,16,128]{4,3,2,1,0:T(8,128)(2,1)S(1)}, bf16[1,16,2,16,128]{4,3,2,1,0:T(8,128)(2,1)S(1)}, u32[]{:S(2)}, u32[]{:S(2)}) collective-permute-start(bf16[1,16,2,16,128]{4,3,2,1,0:T(8,128)(2,1)S(1)} %bitcast.129), channel_id=1, source_target_pairs={{0,10},{2,12},{4,14},{6,0},{8,2},{10,4},{12,6},{14,8},{1,11},{3,13... | collective-permute-start | bytes 393224 | tf_op jit(solution)/shard_map/ppermute | solution.py:40
  74.3 1.5 %collective-permute-start.5 = (bf16[1,16,2,16,128]{4,3,2,1,0:T(8,128)(2,1)S(1)}, bf16[1,16,2,16,128]{4,3,2,1,0:T(8,128)(2,1)S(1)}, u32[]{:S(2)}, u32[]{:S(2)}) collective-permute-start(bf16[1,16,2,16,128]{4,3,2,1,0:T(8,128)(2,1)S(1)} %bitcast.128), channel_id=1, source_target_pairs={{0,12},{2,14},{4,0},{6,2},{8,4},{10,6},{12,8},{14,10},{1,13},{3,15... | collective-permute-start | bytes 393224 | tf_op jit(solution)/shard_map/ppermute | solution.py:40
  75.8 1.9 %collective-permute-start.6 = (bf16[1,16,2,16,128]{4,3,2,1,0:T(8,128)(2,1)S(1)}, bf16[1,16,2,16,128]{4,3,2,1,0:T(8,128)(2,1)S(1)}, u32[]{:S(2)}, u32[]{:S(2)}) collective-permute-start(bf16[1,16,2,16,128]{4,3,2,1,0:T(8,128)(2,1)S(1)} %bitcast.127), channel_id=1, source_target_pairs={{0,14},{2,0},{4,2},{6,4},{8,6},{10,8},{12,10},{14,12},{1,15},{3,1}... | collective-permute-start | bytes 393224 | tf_op jit(solution)/shard_map/ppermute | solution.py:40
  77.8 6.6 %collective-permute-done.2 = bf16[1,16,2,16,128]{4,3,2,1,0:T(8,128)(2,1)S(1)} collective-permute-done((bf16[1,16,2,16,128]{4,3,2,1,0:T(8,128)(2,1)S(1)}, bf16[1,16,2,16,128]{4,3,2,1,0:T(8,128)(2,1)S(1)}, u32[]{:S(2)}, u32[]{:S(2)}) %collective-permute-start.2) | collective-permute-done | bytes 131104 | tf_op jit(solution)/shard_map/ppermute | solution.py:40
  85.1 0.7 gather_fusion.3
  86.5 3.5 %while.16 = (s32[]{:T(128)}, f32[1,128]{1,0:T(1,128)S(1)}, bf16[1,128,2,2048]{3,1,2,0:T(8,128)(2,1)S(1)}, s32[]{:T(128)}, s32[]{:T(128)}, /*index=5*/s32[]{:T(128)}) while((s32[]{:T(128)}, f32[1,128]{1,0:T(1,128)S(1)}, bf16[1,128,2,2048]{3,1,2,0:T(8,128)(2,1)S(1)}, s32[]{:T(128)}, s32[]{:T(128)}, /*index=5*/s32[]{:T(128)}) %tuple.69), condition=%wide.region_4.5_spmd.clone, body=%wide.region_1.4_spmd.clone.sunk | while | flops 539607296 | bytes 12078183 | solution.py:120
  90.0 27.7 %pmax.7 = f32[1,128]{1,0:T(1,128)S(1)} all-reduce(f32[1,128]{1,0:T(1,128)S(1)} %get-tuple-element.113), channel_id=1, replica_groups=mesh['batch'=2,'freq'=8,'elem'=2] {'freq'}, use_global_device_ids=true, to_apply=%region_5.6 | all-reduce | flops 128 | bytes 1024 | tf_op jit(solution)/shard_map/pmax | solution.py:170
  (81 shorter events, 12.3 us)
Async XLA Ops:
  7.2 12.7 %copy-start = (f32[256,256]{1,0:T(8,128)S(1)}, f32[256,256]{1,0:T(8,128)}, u32[]{:S(2)}) copy-start(f32[256,256]{1,0:T(8,128)} %param.13) | copy-start | bytes 786436
  7.2 55.0 %all-reduce.3.cloned.1.call-start = ((), (), s32[]{:S(2)}) async-start(), calls=%async_computation | async-start | bytes 4194304
  8.6 3.5 %copy-start.2 = (s32[8]{0:T(128)S(1)}, s32[8]{0:T(128)}, u32[]{:S(2)}) copy-start(s32[8]{0:T(128)} %param.11) | copy-start | bytes 100
  18.6 0.7 copy-start.3
  38.1 0.7 copy-start.4
  64.5 9.8 %collective-permute-start = (bf16[1,16,2,16,128]{4,3,2,1,0:T(8,128)(2,1)S(1)}, bf16[1,16,2,16,128]{4,3,2,1,0:T(8,128)(2,1)S(1)}, u32[]{:S(2)}, u32[]{:S(2)}) collective-permute-start(bf16[1,16,2,16,128]{4,3,2,1,0:T(8,128)(2,1)S(1)} %bitcast.133), channel_id=1, source_target_pairs={{0,2},{2,4},{4,6},{6,8},{8,10},{10,12},{12,14},{14,0},{1,3},{3,5},... | collective-permute-start | bytes 393224 | tf_op jit(solution)/shard_map/ppermute | solution.py:40
  66.3 9.6 %collective-permute-start.1 = (bf16[1,16,2,16,128]{4,3,2,1,0:T(8,128)(2,1)S(1)}, bf16[1,16,2,16,128]{4,3,2,1,0:T(8,128)(2,1)S(1)}, u32[]{:S(2)}, u32[]{:S(2)}) collective-permute-start(bf16[1,16,2,16,128]{4,3,2,1,0:T(8,128)(2,1)S(1)} %bitcast.132), channel_id=1, source_target_pairs={{0,4},{2,6},{4,8},{6,10},{8,12},{10,14},{12,0},{14,2},{1,5},{3,7},... | collective-permute-start | bytes 393224 | tf_op jit(solution)/shard_map/ppermute | solution.py:40
  67.8 16.5 %collective-permute-start.2 = (bf16[1,16,2,16,128]{4,3,2,1,0:T(8,128)(2,1)S(1)}, bf16[1,16,2,16,128]{4,3,2,1,0:T(8,128)(2,1)S(1)}, u32[]{:S(2)}, u32[]{:S(2)}) collective-permute-start(bf16[1,16,2,16,128]{4,3,2,1,0:T(8,128)(2,1)S(1)} %bitcast.131), channel_id=1, source_target_pairs={{0,6},{2,8},{4,10},{6,12},{8,14},{10,0},{12,2},{14,4},{1,7},{3,9},... | collective-permute-start | bytes 393224 | tf_op jit(solution)/shard_map/ppermute | solution.py:40
  70.3 14.7 %collective-permute-start.3 = (bf16[1,16,2,16,128]{4,3,2,1,0:T(8,128)(2,1)S(1)}, bf16[1,16,2,16,128]{4,3,2,1,0:T(8,128)(2,1)S(1)}, u32[]{:S(2)}, u32[]{:S(2)}) collective-permute-start(bf16[1,16,2,16,128]{4,3,2,1,0:T(8,128)(2,1)S(1)} %bitcast.130), channel_id=1, source_target_pairs={{0,8},{2,10},{4,12},{6,14},{8,0},{10,2},{12,4},{14,6},{1,9},{3,11}... | collective-permute-start | bytes 393224 | tf_op jit(solution)/shard_map/ppermute | solution.py:40
  71.8 13.2 %collective-permute-start.4 = (bf16[1,16,2,16,128]{4,3,2,1,0:T(8,128)(2,1)S(1)}, bf16[1,16,2,16,128]{4,3,2,1,0:T(8,128)(2,1)S(1)}, u32[]{:S(2)}, u32[]{:S(2)}) collective-permute-start(bf16[1,16,2,16,128]{4,3,2,1,0:T(8,128)(2,1)S(1)} %bitcast.129), channel_id=1, source_target_pairs={{0,10},{2,12},{4,14},{6,0},{8,2},{10,4},{12,6},{14,8},{1,11},{3,13... | collective-permute-start | bytes 393224 | tf_op jit(solution)/shard_map/ppermute | solution.py:40
  74.3 10.7 %collective-permute-start.5 = (bf16[1,16,2,16,128]{4,3,2,1,0:T(8,128)(2,1)S(1)}, bf16[1,16,2,16,128]{4,3,2,1,0:T(8,128)(2,1)S(1)}, u32[]{:S(2)}, u32[]{:S(2)}) collective-permute-start(bf16[1,16,2,16,128]{4,3,2,1,0:T(8,128)(2,1)S(1)} %bitcast.128), channel_id=1, source_target_pairs={{0,12},{2,14},{4,0},{6,2},{8,4},{10,6},{12,8},{14,10},{1,13},{3,15... | collective-permute-start | bytes 393224 | tf_op jit(solution)/shard_map/ppermute | solution.py:40
  75.8 9.2 %collective-permute-start.6 = (bf16[1,16,2,16,128]{4,3,2,1,0:T(8,128)(2,1)S(1)}, bf16[1,16,2,16,128]{4,3,2,1,0:T(8,128)(2,1)S(1)}, u32[]{:S(2)}, u32[]{:S(2)}) collective-permute-start(bf16[1,16,2,16,128]{4,3,2,1,0:T(8,128)(2,1)S(1)} %bitcast.127), channel_id=1, source_target_pairs={{0,14},{2,0},{4,2},{6,4},{8,6},{10,8},{12,10},{14,12},{1,15},{3,1}... | collective-permute-start | bytes 393224 | tf_op jit(solution)/shard_map/ppermute | solution.py:40
  86.5 31.3 %copy-start.1 = (f32[1,16]{1,0:T(1,128)S(1)}, f32[1,16]{1,0:T(1,128)}, u32[]{:S(2)}) copy-start(f32[1,16]{1,0:T(1,128)} %param.17) | copy-start | bytes 196
Sparse Core Ops, SparseCore 0:
  38.3 23.9 all-reduce.2
